TPU v7x, 256 devices: a whole 4x4x8 slice. The times are simulated.
256 devices in a mesh: row: 16 (over y, z_lo, core), col: 16 (over z_hi, x).
Axes of the slice: x: 4, y: 4, z: 8 (z_hi: 4, z_lo: 2; z = z_hi * 2 + z_lo), core: 2. Of those that a mesh axis runs over, the one named last changes fastest.
Arguments:
- pairs: bfloat16 [2, 256, 20480], P(None, None, ('row', 'col')), may hold values from -12 to 12
- prior: bfloat16 [2, 20480, 20480], P(None, 'row', 'col'), may hold values from -0.025146484 to 0.025146484
- val_band: int32 [256], replicated, may hold values from 0 to 255
- cond_band: int32 [256], replicated, may hold values from 0 to 2047
- val_energy: float32 [256], replicated, may hold values from -3 to -1
- cond_energy: float32 [2048], replicated, may hold values from 0.5 to 2.5
- coul_root: float32 [20480], replicated, may hold values from 0.3 to 1.5
- potential: float32 [2, 128, 20480], P(None, 'col', 'row'), may hold values from -6 to 6
Outputs:
- screened: float32 [2, 128, 20480], P(None, 'col', 'row')
All inputs are finite; a program needn't handle non-finite values.
Results may differ from a plain program's by a relative error of at most 0.0007.
Values may be sent and summed in bfloat16 or wider, within the bound.
No kernel may reach another device: no remote copies, remote signals or barrier semaphores. Data moves between devices by JAX's collectives and lax.ppermute only.
A program may use at most 128 MiB of HBM per device.

v0:
```python
import jax
import jax.numpy as jnp
from jax import lax
from jax.sharding import PartitionSpec as P

NG = 20480
ITERS = 2


def spread(block, axis, holder):
    block = jnp.where(lax.axis_index(axis) == holder, block, jnp.zeros_like(block))
    return lax.psum(block, axis)


def contract_pairs(first, second):
    return lax.dot_general(
        first, second, (((0,), (0,)), ((), ())), preferred_element_type=jnp.float32
    )


def through(scaled_part, matrix):
    return lax.dot_general(
        scaled_part,
        matrix,
        (((1,), (1,)), ((), ())),
        precision=lax.Precision.HIGHEST,
        preferred_element_type=jnp.float32,
    )


def pick_energy(band, energy):
    levels = jnp.arange(energy.shape[0], dtype=jnp.int32)
    return jnp.sum(jnp.where(band[:, None] == levels[None, :], energy[None, :], 0.0), axis=1)


def column_values(gathered, gain_row, source_row):
    scaled = gathered * gain_row[None, None, :]
    return spread(scaled, "row", source_row)


def respond(scaled_cols, response_real, response_imag):
    real_part = through(scaled_cols[0], response_real) - through(scaled_cols[1], response_imag)
    imag_part = through(scaled_cols[0], response_imag) + through(scaled_cols[1], response_real)
    return jnp.stack([real_part, imag_part])


def local(pairs, prior, val_band, cond_band, val_energy, cond_energy, coul_root, potential):
    row_count = lax.axis_size("row")
    col_count = lax.axis_size("col")
    row_index = lax.axis_index("row")
    col_index = lax.axis_index("col")
    row_width = prior.shape[1]
    source_row = col_index * row_count // col_count
    weights = 1.0 / (pick_energy(cond_band, cond_energy) - pick_energy(val_band, val_energy))
    row_pairs = lax.all_gather(pairs, "col", axis=2, tiled=True)
    col_pairs = spread(row_pairs, "row", source_row)
    weighted = (weights[None, :, None] * col_pairs.astype(jnp.float32)).astype(jnp.bfloat16)
    left_stack = jnp.concatenate([row_pairs[0], row_pairs[1]], axis=0)
    right_stack = jnp.concatenate([weighted[0], weighted[1]], axis=0)
    response_real = prior[0].astype(jnp.float32) + contract_pairs(left_stack, right_stack) / NG
    left_other = jnp.concatenate([row_pairs[0], -row_pairs[1]], axis=0)
    right_other = jnp.concatenate([weighted[1], weighted[0]], axis=0)
    response_imag = prior[1].astype(jnp.float32) + contract_pairs(left_other, right_other) / NG
    gain_row = lax.dynamic_slice_in_dim(coul_root, row_index * row_width, row_width, 0)
    iterate = potential
    for _ in range(ITERS):
        gathered = lax.all_gather(iterate, "col", axis=1, tiled=True)
        scaled_cols = column_values(gathered, gain_row, source_row)
        partial_value = respond(scaled_cols, response_real, response_imag)
        summed = lax.psum_scatter(partial_value, "col", scatter_dimension=1, tiled=True)
        applied = iterate + gain_row[None, None, :] * summed
        iterate = iterate + 0.5 * (potential - applied)
    return iterate


def solution(mesh):
    in_specs = (
        P(None, None, ("row", "col")),
        P(None, "row", "col"),
        P(),
        P(),
        P(),
        P(),
        P(),
        P(None, "col", "row"),
    )
    out_specs = P(None, "col", "row")
    return jax.shard_map(local, mesh=mesh, in_specs=in_specs, out_specs=out_specs, check_vma=False)
```

profile of v0, /device:TPU:8, one launch (start us, length us, event | category | flops | bytes accessed | tf_op | source)
XLA Modules:
  0.0 811.0 jit_solution(6735044136014977329)
XLA Ops:
  8.1 58.8 %all-gather.6.cloned.1.call-done = bf16[2,256,1280]{1,2,0:T(8,128)(2,1)} async-done(((bf16[2,256,80]{1,2,0:T(8,128)(2,1)}), bf16[2,256,1280]{1,2,0:T(8,128)(2,1)}) %all-gather.6.cloned.1.call-update) | async-done | bytes 1310736 | tf_op jit(solution)/shard_map/all_gather | solution.py:55
  69.6 51.5 %all-gather.4.cloned.1.call-done = f32[2,128,1280]{2,1,0:T(8,128)} async-done(((f32[2,8,1280]{2,1,0:T(8,128)}), f32[2,128,1280]{2,1,0:T(8,128)}) %all-gather.4.cloned.1.call-update) | async-done | bytes 1310736 | tf_op jit(solution)/shard_map/all_gather | solution.py:67
  121.1 2.5 multiply_select_fusion.1
  123.6 1.2 copy-done.1
  125.0 116.9 %all-reduce.6.cloned.1.call-done = bf16[2,256,1280]{1,2,0:T(8,128)(2,1)} async-done(((bf16[2,256,1280]{1,2,0:T(8,128)(2,1)}), bf16[2,256,1280]{1,2,0:T(8,128)(2,1)}) %all-reduce.6.cloned.1.call-update) | async-done | bytes 1310736 | tf_op jit(solution)/shard_map/psum | solution.py:12
  241.9 1.6 multiply_convert_fusion
  243.6 6.7 fusion.1
  250.3 4.7 fusion
  255.0 115.7 %all-reduce.4.cloned.1.call-done = f32[2,128,1280]{2,1,0:T(8,128)} async-done(((f32[2,128,1280]{2,1,0:T(8,128)}), f32[2,128,1280]{2,1,0:T(8,128)}) %all-reduce.4.cloned.1.call-update) | async-done | bytes 1310736 | tf_op jit(solution)/shard_map/psum | solution.py:12
  370.7 9.9 %fusion.14 = f32[128,1280]{1,0:T(8,128)S(1)} fusion(f32[1280,1280]{1,0:T(8,128)} %fusion.1, f32[2,128,1280]{2,1,0:T(8,128)} %all-reduce.4.cloned.1.call-done), kind=kOutput, calls=%fused_computation.38 | convolution fusion | flops 2516582400 | bytes 7864320 | tf_op jit(solution)/shard_map/dot_general | solution.py:22
  380.7 6.9 fusion.15
  387.6 6.8 fusion.3
  394.4 7.0 fusion.2
  402.7 93.3 %reduce-scatter.3.cloned.1.call-done = f32[2,8,1280]{2,1,0:T(8,128)} async-done(((f32[2,128,1280]{2,1,0:T(8,128)}), f32[2,8,1280]{2,1,0:T(8,128)}) %reduce-scatter.3.cloned.1.call-update) | async-done | bytes 81936 | tf_op jit(solution)/shard_map/reduce_scatter | solution.py:70
  496.0 1.5 fusion.19
  497.6 52.5 %all-gather.8.cloned.1.call-done = f32[2,128,1280]{2,1,0:T(8,128)} async-done(((f32[2,8,1280]{2,1,0:T(8,128)}), f32[2,128,1280]{2,1,0:T(8,128)}) %all-gather.8.cloned.1.call-update) | async-done | bytes 1310736 | tf_op jit(solution)/shard_map/all_gather | solution.py:67
  550.1 2.5 multiply_select_fusion
  552.7 118.3 %all-reduce.8.cloned.1.call-done = f32[2,128,1280]{2,1,0:T(8,128)} async-done(((f32[2,128,1280]{2,1,0:T(8,128)}), f32[2,128,1280]{2,1,0:T(8,128)}) %all-reduce.8.cloned.1.call-update) | async-done | bytes 1310736 | tf_op jit(solution)/shard_map/psum | solution.py:12
  671.0 9.9 %fusion.16 = f32[128,1280]{1,0:T(8,128)S(1)} fusion(f32[1280,1280]{1,0:T(8,128)} %fusion.1, f32[2,128,1280]{2,1,0:T(8,128)} %all-reduce.8.cloned.1.call-done), kind=kOutput, calls=%fused_computation.40 | convolution fusion | flops 2516582400 | bytes 7864320 | tf_op jit(solution)/shard_map/dot_general | solution.py:22
  680.9 9.8 %fusion.17 = f32[128,1280]{1,0:T(8,128)S(1)} fusion(f32[1280,1280]{1,0:T(8,128)} %fusion, f32[2,128,1280]{2,1,0:T(8,128)S(1)} %copy-done.3), kind=kOutput, calls=%fused_computation.41 | convolution fusion | flops 2516582400 | bytes 7864320 | tf_op jit(solution)/shard_map/dot_general | solution.py:22
  690.7 10.0 %fusion.5 = f32[1,128,1280]{2,1,0:T(8,128)S(1)} fusion(f32[128,1280]{1,0:T(8,128)S(1)} %fusion.16, f32[1280,1280]{1,0:T(8,128)} %fusion, f32[2,128,1280]{2,1,0:T(8,128)S(1)} %copy-done.3), kind=kOutput, calls=%fused_computation.12 | convolution fusion | flops 2516746240 | bytes 8519680 | tf_op jit(solution)/shard_map/dot_general | solution.py:22
  700.8 6.8 fusion.4
  708.7 93.4 %reduce-scatter.5.cloned.1.call-done = f32[2,8,1280]{2,1,0:T(8,128)} async-done(((f32[2,128,1280]{2,1,0:T(8,128)}), f32[2,8,1280]{2,1,0:T(8,128)}) %reduce-scatter.5.cloned.1.call-update) | async-done | bytes 81936 | tf_op jit(solution)/shard_map/reduce_scatter | solution.py:70
  802.1 1.6 multiply_add_fusion
  (60 shorter events, 6.9 us)
Async XLA Ops:
  6.5 60.4 %all-gather.6.cloned.1.call-start = ((), (), s32[]{:S(2)}) async-start(), calls=%async_computation.4 | async-start | bytes 1392640 | tf_op jit(solution)/shard_map/all_gather | solution.py:55
  7.3 113.8 %all-gather.4.cloned.1.call-start = ((), (), s32[]{:S(2)}) async-start(), calls=%async_computation.2 | async-start | bytes 1392640 | tf_op jit(solution)/shard_map/all_gather | solution.py:67
  8.0 233.9 %all-reduce.6.cloned.1.call-start = ((), (), s32[]{:S(2)}) async-start(), calls=%async_computation.5 | async-start | bytes 2621440 | tf_op jit(solution)/shard_map/psum | solution.py:12
  68.1 0.9 copy-start.7
  68.1 0.9 copy-start.8
  68.1 1.1 copy-start.6
  68.1 1.1 copy-start.9
  68.1 302.6 %all-reduce.4.cloned.1.call-start = ((), (), s32[]{:S(2)}) async-start(), calls=%async_computation.3 | async-start | bytes 2621440 | tf_op jit(solution)/shard_map/psum | solution.py:12
  123.5 1.3 copy-start.1
  123.6 372.4 %reduce-scatter.3.cloned.1.call-start = ((), (), s32[]{:S(2)}) async-start(), calls=%async_computation.6 | async-start | bytes 1392640 | tf_op jit(solution)/shard_map/reduce_scatter | solution.py:70
  243.5 6.8 slice-start.4
  243.6 6.7 slice-start.5
  370.7 10.0 %copy-start = (f32[1280,1280]{1,0:T(8,128)S(1)}, f32[1280,1280]{1,0:T(8,128)}, u32[]{:S(2)}) copy-start(f32[1280,1280]{1,0:T(8,128)} %fusion) | copy-start | bytes 19660804
  370.7 10.0 %copy-start.2 = (f32[2,128,1280]{2,1,0:T(8,128)S(1)}, f32[2,128,1280]{2,1,0:T(8,128)}, u32[]{:S(2)}) copy-start(f32[2,128,1280]{2,1,0:T(8,128)} %all-reduce.4.cloned.1.call-done) | copy-start | bytes 3932164
  380.7 13.7 %slice-start = ((s8[6553600]{0:T(1024)(128)(4,1)}), s8[4194304]{0:T(1024)(128)(4,1)S(1)}, s32[]{:S(2)}) async-start(s8[6553600]{0:T(1024)(128)(4,1)} %bitcast.48), calls=%async_computation.10 | async-start | bytes 8388608
  387.6 6.8 slice-start.1
  402.6 93.4 %copy-start.4 = (f32[2,8,1280]{2,1,0:T(8,128)S(1)}, f32[2,8,1280]{2,1,0:T(8,128)}, u32[]{:S(2)}) copy-start(f32[2,8,1280]{2,1,0:T(8,128)} %param.15) | copy-start | bytes 245764
  402.6 147.5 %all-gather.8.cloned.1.call-start = ((), (), s32[]{:S(2)}) async-start(), calls=%async_computation.7 | async-start | bytes 1392640 | tf_op jit(solution)/shard_map/all_gather | solution.py:67
  497.6 173.4 %all-reduce.8.cloned.1.call-start = ((), (), s32[]{:S(2)}) async-start(), calls=%async_computation.8 | async-start | bytes 2621440 | tf_op jit(solution)/shard_map/psum | solution.py:12
  552.6 249.5 %reduce-scatter.5.cloned.1.call-start = ((), (), s32[]{:S(2)}) async-start(), calls=%async_computation.9 | async-start | bytes 1392640 | tf_op jit(solution)/shard_map/reduce_scatter | solution.py:70
  671.0 9.9 %copy-start.3 = (f32[2,128,1280]{2,1,0:T(8,128)S(1)}, f32[2,128,1280]{2,1,0:T(8,128)}, u32[]{:S(2)}) copy-start(f32[2,128,1280]{2,1,0:T(8,128)} %all-reduce.8.cloned.1.call-done) | copy-start | bytes 3932164
  680.9 19.8 %slice-start.2 = ((s8[6553600]{0:T(1024)(128)(4,1)}), s8[4194304]{0:T(1024)(128)(4,1)S(1)}, s32[]{:S(2)}) async-start(s8[6553600]{0:T(1024)(128)(4,1)} %bitcast.50), calls=%async_computation.12 | async-start | bytes 8388608
  690.7 10.1 %slice-start.3 = ((s8[6553600]{0:T(1024)(128)(4,1)}), s8[2359296]{0:T(1024)(128)(4,1)S(1)}, s32[]{:S(2)}) async-start(s8[6553600]{0:T(1024)(128)(4,1)} %bitcast.50), calls=%async_computation.13 | async-start | bytes 4718592
  708.7 93.4 %copy-start.5 = (f32[2,8,1280]{2,1,0:T(8,128)S(1)}, f32[2,8,1280]{2,1,0:T(8,128)}, u32[]{:S(2)}) copy-start(f32[2,8,1280]{2,1,0:T(8,128)} %reduce-scatter.3.cloned.1.call-done) | copy-start | bytes 245764
Sparse Core Ops, SparseCore 0:
  9.8 57.1 all-gather.5
  69.3 51.6 all-gather.3
  123.7 118.1 all-reduce.5
  244.4 126.2 all-reduce.3
  402.7 93.2 reduce-scatter.2
  498.3 51.7 all-gather.7
  552.8 118.1 all-reduce.7
  708.9 93.2 reduce-scatter.4
where the time goes:
time: 820 us; the launch traced here: 811 us
  waiting for transfers between devices  702 us (86%)
  matrix products  78.5 us (10%)
  between operations  14.2 us (2%)
  other arithmetic  13.7 us (2%)
    psum x3, waiting for transfers between devices, spread(): return lax.psum(block, axis)  351 us
    reduce_scatter x2, waiting for transfers between devices, local(): lax.psum_scatter(partial_value, 'col', scatter_dimension=1, tiled=True)  187 us
    all_gather x2, waiting for transfers between devices, local(): gathered = lax.all_gather(iterate, 'col', axis=1, tiled=True)  104 us
    dot_general x8, matrix products, through(): lax.dot_general(scaled_part, matrix, (((1,), (1,)), ((), ())), precision=...  67.1 us
    all_gather x1, waiting for transfers between devices, local(): row_pairs = lax.all_gather(pairs, 'col', axis=2, tiled=True)  58.8 us
  transfers between devices with their start and end apart: 8, of which 8 were waited for; matrix products, arithmetic and copies ran while one was open for 2% of the time, Pallas kernels for 0%

commit v1 on v0

--- a/solution.py
+++ b/solution.py
@@ -1,3 +1,4 @@
+import functools
 import jax
 import jax.numpy as jnp
 from jax import lax
@@ -5,6 +6,16 @@
 
 NG = 20480
 ITERS = 2
+
+
+def _guide_sources_all(vec, array_axis, lane_axis):
+    r1 = lax.axis_size(lane_axis)
+    local_out = jnp.stack(r1 * [vec], axis=0)
+    x_now = lax.all_to_all(local_out, lane_axis, 0, 0)
+    return jnp.concatenate(x_now, axis=array_axis)
+
+
+compute_roads = functools.partial(_guide_sources_all, array_axis=1, lane_axis="col")
 
 
 def spread(block, axis, holder):
@@ -64,7 +75,7 @@
     gain_row = lax.dynamic_slice_in_dim(coul_root, row_index * row_width, row_width, 0)
     iterate = potential
     for _ in range(ITERS):
-        gathered = lax.all_gather(iterate, "col", axis=1, tiled=True)
+        gathered = compute_roads(iterate)
         scaled_cols = column_values(gathered, gain_row, source_row)
         partial_value = respond(scaled_cols, response_real, response_imag)
         summed = lax.psum_scatter(partial_value, "col", scatter_dimension=1, tiled=True)

time: 820 us -> 759 us (0.926)
  waiting for transfers between devices: 702 us -> 591 us
  blocking collectives: 0 us -> 38.8 us
  starting transfers between devices: 0.29 us -> 11.2 us
    all_gather x2 -> x0, waiting for transfers between devices: 104 us -> none  [local(): gathered = lax.all_gather(iterate, 'col', axis=1, tiled=True)]
    all_to_all x0 -> x1, blocking collectives: none -> 38.8 us  [_guide_sources_all(): x_now = lax.all_to_all(local_out, lane_axis, 0, 0)]
    all_to_all x0 -> x1, starting transfers between devices: none -> 11 us  [_guide_sources_all(): x_now = lax.all_to_all(local_out, lane_axis, 0, 0)]
  transfers between devices with their start and end apart: 8 -> 7, of which waited for: 8 -> 6; matrix products, arithmetic and copies ran while one was open for 2% -> 3% of each run, Pallas kernels for 0% -> 0%
where the time goes in v1:
time: 759 us; the launch traced here: 749 us
  waiting for transfers between devices  591 us (78%)
  matrix products  78.5 us (10%)
  blocking collectives  38.8 us (5%)
  between operations  14.2 us (2%)
  starting transfers between devices  11.2 us (1%)
  other arithmetic  10.5 us (1%)
    psum x3, waiting for transfers between devices, spread(): return lax.psum(block, axis)  349 us
    reduce_scatter x2, waiting for transfers between devices, local(): lax.psum_scatter(partial_value, 'col', scatter_dimension=1, tiled=True)  187 us
    dot_general x8, matrix products, through(): lax.dot_general(scaled_part, matrix, (((1,), (1,)), ((), ())), precision=...  67.1 us
    all_gather x1, waiting for transfers between devices, local(): row_pairs = lax.all_gather(pairs, 'col', axis=2, tiled=True)  54.7 us
    all_to_all x1, blocking collectives, _guide_sources_all(): x_now = lax.all_to_all(local_out, lane_axis, 0, 0)  38.8 us
  transfers between devices with their start and end apart: 7, of which 6 were waited for; matrix products, arithmetic and copies ran while one was open for 3% of the time, Pallas kernels for 0%

profile of v1, /device:TPU:8, one launch (start us, length us, event | category | flops | bytes accessed | tf_op | source)
XLA Modules:
  0.0 748.9 jit_solution(1501274487878529633)
XLA Ops:
  7.3 2.1 stack.16
  9.3 11.0 %all-to-all-start = ((f32[16,2,8,1280]{3,2,1,0:T(8,128)}), f32[16,2,8,1280]{3,2,1,0:T(8,128)S(1)}, u32[]{:S(2)}, u32[]{:S(2)}) async-start(f32[16,2,8,1280]{3,2,1,0:T(8,128)} %stack.16), calls=%async_computation | async-start | bytes 2621440 | tf_op jit(solution)/shard_map/all_to_all | solution.py:14
  20.4 54.7 %all-gather.2.cloned.1.call-done = bf16[2,256,1280]{1,2,0:T(8,128)(2,1)} async-done(((bf16[2,256,80]{1,2,0:T(8,128)(2,1)}), bf16[2,256,1280]{1,2,0:T(8,128)(2,1)}) %all-gather.2.cloned.1.call-update) | async-done | bytes 1310736 | tf_op jit(solution)/shard_map/all_gather | solution.py:66
  77.8 1.2 fusion.15
  79.1 1.2 copy-done.1
  80.5 115.6 %all-reduce.6.cloned.1.call-done = bf16[2,256,1280]{1,2,0:T(8,128)(2,1)} async-done(((bf16[2,256,1280]{1,2,0:T(8,128)(2,1)}), bf16[2,256,1280]{1,2,0:T(8,128)(2,1)}) %all-reduce.6.cloned.1.call-update) | async-done | bytes 1310736 | tf_op jit(solution)/shard_map/psum | solution.py:23
  196.1 1.6 multiply_convert_fusion
  197.8 6.7 fusion.1
  204.5 4.7 fusion
  209.1 115.9 %all-reduce.4.cloned.1.call-done = f32[2,128,1280]{2,1,0:T(8,128)} async-done(((f32[2,128,1280]{2,1,0:T(8,128)}), f32[2,128,1280]{2,1,0:T(8,128)}) %all-reduce.4.cloned.1.call-update) | async-done | bytes 1310736 | tf_op jit(solution)/shard_map/psum | solution.py:23
  325.0 9.9 %fusion.16 = f32[128,1280]{1,0:T(8,128)S(1)} fusion(f32[1280,1280]{1,0:T(8,128)} %fusion.1, f32[2,128,1280]{2,1,0:T(8,128)} %all-reduce.4.cloned.1.call-done), kind=kOutput, calls=%fused_computation.40 | convolution fusion | flops 2516582400 | bytes 7864320 | tf_op jit(solution)/shard_map/dot_general | solution.py:33
  335.0 6.9 fusion.17
  341.9 6.8 fusion.3
  348.7 7.0 fusion.2
  357.0 93.4 %reduce-scatter.3.cloned.1.call-done = f32[2,8,1280]{2,1,0:T(8,128)} async-done(((f32[2,128,1280]{2,1,0:T(8,128)}), f32[2,8,1280]{2,1,0:T(8,128)}) %reduce-scatter.3.cloned.1.call-update) | async-done | bytes 81936 | tf_op jit(solution)/shard_map/reduce_scatter | solution.py:81
  451.4 38.8 %all_to_all.10 = f32[16,2,8,1280]{3,2,1,0:T(8,128)S(1)} all-to-all(f32[16,2,8,1280]{3,2,1,0:T(8,128)S(1)} %stack.20), channel_id=1, replica_groups=mesh['row'=16,'col'=16] {'col'}, dimensions={0} | all-to-all | bytes 2621440 | tf_op jit(solution)/shard_map/all_to_all | solution.py:14
  490.2 1.2 fusion.14
  491.4 117.4 %all-reduce.8.cloned.1.call-done = f32[2,128,1280]{2,1,0:T(8,128)} async-done(((f32[2,128,1280]{2,1,0:T(8,128)}), f32[2,128,1280]{2,1,0:T(8,128)}) %all-reduce.8.cloned.1.call-update) | async-done | bytes 1310736 | tf_op jit(solution)/shard_map/psum | solution.py:23
  608.8 9.9 %fusion.18 = f32[128,1280]{1,0:T(8,128)S(1)} fusion(f32[1280,1280]{1,0:T(8,128)} %fusion.1, f32[2,128,1280]{2,1,0:T(8,128)} %all-reduce.8.cloned.1.call-done), kind=kOutput, calls=%fused_computation.42 | convolution fusion | flops 2516582400 | bytes 7864320 | tf_op jit(solution)/shard_map/dot_general | solution.py:33
  618.8 9.8 %fusion.19 = f32[128,1280]{1,0:T(8,128)S(1)} fusion(f32[1280,1280]{1,0:T(8,128)} %fusion, f32[2,128,1280]{2,1,0:T(8,128)S(1)} %copy-done.3), kind=kOutput, calls=%fused_computation.43 | convolution fusion | flops 2516582400 | bytes 7864320 | tf_op jit(solution)/shard_map/dot_general | solution.py:33
  628.5 10.0 %fusion.5 = f32[1,128,1280]{2,1,0:T(8,128)S(1)} fusion(f32[128,1280]{1,0:T(8,128)S(1)} %fusion.18, f32[1280,1280]{1,0:T(8,128)} %fusion, f32[2,128,1280]{2,1,0:T(8,128)S(1)} %copy-done.3), kind=kOutput, calls=%fused_computation.12 | convolution fusion | flops 2516746240 | bytes 8519680 | tf_op jit(solution)/shard_map/dot_general | solution.py:33
  638.6 6.8 fusion.4
  646.6 93.5 %reduce-scatter.5.cloned.1.call-done = f32[2,8,1280]{2,1,0:T(8,128)} async-done(((f32[2,128,1280]{2,1,0:T(8,128)}), f32[2,8,1280]{2,1,0:T(8,128)}) %reduce-scatter.5.cloned.1.call-update) | async-done | bytes 81936 | tf_op jit(solution)/shard_map/reduce_scatter | solution.py:81
  740.0 1.6 multiply_add_fusion
  (59 shorter events, 7.1 us)
Async XLA Ops:
  6.5 68.6 %all-gather.2.cloned.1.call-start = ((), (), s32[]{:S(2)}) async-start(), calls=%async_computation.5 | async-start | bytes 1392640 | tf_op jit(solution)/shard_map/all_gather | solution.py:66
  9.3 68.5 %all-to-all-start = ((f32[16,2,8,1280]{3,2,1,0:T(8,128)}), f32[16,2,8,1280]{3,2,1,0:T(8,128)S(1)}, u32[]{:S(2)}, u32[]{:S(2)}) async-start(f32[16,2,8,1280]{3,2,1,0:T(8,128)} %stack.16), calls=%async_computation | async-start | bytes 2621440 | tf_op jit(solution)/shard_map/all_to_all | solution.py:14
  20.4 175.7 %all-reduce.6.cloned.1.call-start = ((), (), s32[]{:S(2)}) async-start(), calls=%async_computation.6 | async-start | bytes 2621440 | tf_op jit(solution)/shard_map/psum | solution.py:23
  76.3 0.9 copy-start.7
  76.3 0.9 copy-start.8
  76.3 1.1 copy-start.6
  76.3 1.1 copy-start.9
  76.4 248.6 %all-reduce.4.cloned.1.call-start = ((), (), s32[]{:S(2)}) async-start(), calls=%async_computation.4 | async-start | bytes 2621440 | tf_op jit(solution)/shard_map/psum | solution.py:23
  79.0 1.3 copy-start.1
  79.0 371.4 %reduce-scatter.3.cloned.1.call-start = ((), (), s32[]{:S(2)}) async-start(), calls=%async_computation.7 | async-start | bytes 1392640 | tf_op jit(solution)/shard_map/reduce_scatter | solution.py:81
  197.6 6.8 slice-start.4
  197.7 6.7 slice-start.5
  325.0 9.9 %copy-start = (f32[1280,1280]{1,0:T(8,128)S(1)}, f32[1280,1280]{1,0:T(8,128)}, u32[]{:S(2)}) copy-start(f32[1280,1280]{1,0:T(8,128)} %fusion) | copy-start | bytes 19660804
  325.0 10.0 %copy-start.2 = (f32[2,128,1280]{2,1,0:T(8,128)S(1)}, f32[2,128,1280]{2,1,0:T(8,128)}, u32[]{:S(2)}) copy-start(f32[2,128,1280]{2,1,0:T(8,128)} %all-reduce.4.cloned.1.call-done) | copy-start | bytes 3932164
  335.0 13.7 %slice-start = ((s8[6553600]{0:T(1024)(128)(4,1)}), s8[4194304]{0:T(1024)(128)(4,1)S(1)}, s32[]{:S(2)}) async-start(s8[6553600]{0:T(1024)(128)(4,1)} %bitcast.60), calls=%async_computation.10 | async-start | bytes 8388608
  341.9 6.8 slice-start.1
  356.9 93.5 %copy-start.4 = (f32[2,8,1280]{2,1,0:T(8,128)S(1)}, f32[2,8,1280]{2,1,0:T(8,128)}, u32[]{:S(2)}) copy-start(f32[2,8,1280]{2,1,0:T(8,128)} %param.15) | copy-start | bytes 245764
  356.9 251.9 %all-reduce.8.cloned.1.call-start = ((), (), s32[]{:S(2)}) async-start(), calls=%async_computation.8 | async-start | bytes 2621440 | tf_op jit(solution)/shard_map/psum | solution.py:23
  491.4 248.7 %reduce-scatter.5.cloned.1.call-start = ((), (), s32[]{:S(2)}) async-start(), calls=%async_computation.9 | async-start | bytes 1392640 | tf_op jit(solution)/shard_map/reduce_scatter | solution.py:81
  608.8 9.9 %copy-start.3 = (f32[2,128,1280]{2,1,0:T(8,128)S(1)}, f32[2,128,1280]{2,1,0:T(8,128)}, u32[]{:S(2)}) copy-start(f32[2,128,1280]{2,1,0:T(8,128)} %all-reduce.8.cloned.1.call-done) | copy-start | bytes 3932164
  618.7 19.8 %slice-start.2 = ((s8[6553600]{0:T(1024)(128)(4,1)}), s8[4194304]{0:T(1024)(128)(4,1)S(1)}, s32[]{:S(2)}) async-start(s8[6553600]{0:T(1024)(128)(4,1)} %bitcast.62), calls=%async_computation.12 | async-start | bytes 8388608
  628.5 10.1 %slice-start.3 = ((s8[6553600]{0:T(1024)(128)(4,1)}), s8[2359296]{0:T(1024)(128)(4,1)S(1)}, s32[]{:S(2)}) async-start(s8[6553600]{0:T(1024)(128)(4,1)} %bitcast.62), calls=%async_computation.13 | async-start | bytes 4718592
  646.5 93.5 %copy-start.5 = (f32[2,8,1280]{2,1,0:T(8,128)S(1)}, f32[2,8,1280]{2,1,0:T(8,128)}, u32[]{:S(2)}) copy-start(f32[2,8,1280]{2,1,0:T(8,128)} %reduce-scatter.3.cloned.1.call-done) | copy-start | bytes 245764
Sparse Core Ops, SparseCore 0:
  9.8 65.3 all-gather.1
  77.8 118.1 all-reduce.5
  198.7 126.2 all-reduce.3
  357.0 93.2 reduce-scatter.2
  491.5 117.2 all-reduce.7
  646.7 93.2 reduce-scatter.4
